TPU v7x, 512 devices: a whole 4x4x16 slice. The times are simulated.
512 devices in a mesh: layer: 16 (over y, x), dp: 32 (over z, core).
Axes of the slice: x: 4, y: 4, z: 16, core: 2. Of those that a mesh axis runs over, the one named last changes fastest.
Arguments:
- inputs: bfloat16 [4096, 1024], P('dp'), may hold values from -6 to 6
- guess_fwd: float32 [16, 4096, 1024], P('layer', 'dp'), may hold values from -9 to 9
- guess_adj: float32 [16, 4096, 1024], P('layer', 'dp'), may hold values from -6 to 6
- weights: bfloat16 [32, 1024, 1024], P('layer', 'dp'), may hold values from -0.1875 to 0.1875
- biases: float32 [32, 1024], P('layer'), may hold values from -3 to 3
- gains: float32 [16, 1024], P('layer'), may hold values from 0.6 to 1
- cotangent: bfloat16 [4096, 1024], P('dp'), may hold values from -6 to 6
Outputs:
- block_ends: float32 [16, 4096, 1024], P('layer', 'dp')
- block_adjoints: float32 [16, 4096, 1024], P('layer', 'dp')
- weight_grad: float32 [32, 1024, 1024], P('layer', 'dp')
- coarse_ends: float32 [16, 4096, 1024], P('layer', 'dp')
- coarse_adjoints: float32 [16, 4096, 1024], P('layer', 'dp')
All inputs are finite; a program needn't handle non-finite values.
Results may differ from a plain program's by a relative error of at most 0.024.
Values may be sent and summed in bfloat16 or wider, within the bound.
No kernel may reach another device: no remote copies, remote signals or barrier semaphores. Data moves between devices by JAX's collectives and lax.ppermute only.
A program may use at most 64 MiB of HBM per device.

v0:
```python
import jax
import jax.numpy as jnp
from jax import lax
from jax.sharding import PartitionSpec as P

step_size = 0.5


def from_behind(block, axis, distance):
    devices = range(lax.axis_size(axis))
    route = [(i - distance, i) for i in devices if i - distance in devices]
    return lax.ppermute(block, axis, route)


def prefix(shard, axis, combine, identity, reverse):
    size, place = (lax.axis_size(axis), lax.axis_index(axis))
    everything = jax.tree.map(lambda part: lax.all_gather(part, axis), shard)
    start = jax.tree.map(
        lambda part, zero: jnp.broadcast_to(jnp.asarray(zero, part.dtype), part.shape),
        shard,
        identity,
    )

    def hop(k, before):
        at = size - 1 - k if reverse else k
        reached = at > place if reverse else at < place
        new = combine(before, jax.tree.map(lambda part: part[at], everything))
        return jax.tree.map(lambda a, b: jnp.where(reached, a, b), new, before)

    return lax.fori_loop(0, size, hop, start)


def combine(earlier, later):
    return (earlier[0] * later[0], earlier[1] * later[0] + later[1])


def forward_block(start, weights, biases):
    state = start
    kept = []
    slopes = []
    for j in range(weights.shape[0]):
        rounded = state.astype(jnp.bfloat16)
        active = jnp.tanh(
            jnp.dot(rounded, weights[j], preferred_element_type=jnp.float32) + biases[j]
        )
        kept.append(rounded)
        slopes.append(1.0 - active * active)
        state = state + step_size * active
    return (state, kept, slopes)


def back_layer(adjoint, weight, slope):
    scaled = (adjoint * slope).astype(jnp.bfloat16)
    moved = lax.dot_general(
        scaled, weight, (((1,), (1,)), ((), ())), preferred_element_type=jnp.float32
    )
    return (adjoint + step_size * moved, scaled)


def backward_block(end, weights, slopes):
    adjoint = end
    for j in reversed(range(weights.shape[0])):
        adjoint = back_layer(adjoint, weights[j], slopes[j])[0]
    return adjoint


def grad_term(kept_rows, scaled):
    return step_size * lax.dot_general(
        kept_rows, scaled, (((0,), (0,)), ((), ())), preferred_element_type=jnp.float32
    )


def local(inputs, guess_fwd, guess_adj, weights, biases, gains, cotangent):
    full_weights = lax.all_gather(weights, "dp", axis=1, tiled=True)
    count = lax.axis_size("layer")
    index = lax.axis_index("layer")
    is_first = index == 0
    is_last = index == count - 1
    anchor = inputs.astype(jnp.float32)
    guess = guess_fwd[0]
    identity = (jnp.ones_like(gains), jnp.zeros_like(guess))
    arrived = from_behind(guess, "layer", 1)
    start = jnp.where(is_first, anchor, arrived)
    end_state = forward_block(start, full_weights, biases)[0]
    resid = end_state - guess
    factor, carried = prefix((gains, resid), "layer", combine, identity, False)
    guess = guess + (gains * carried + resid)
    start = jnp.where(is_first, anchor, from_behind(guess, "layer", 1))
    end_state, kept, slopes = forward_block(start, full_weights, biases)
    final_adj = cotangent.astype(jnp.float32)
    lam = guess_adj[0]
    arrived_adj = from_behind(lam, "layer", -1)
    end_adj = jnp.where(is_last, final_adj, arrived_adj)
    back = backward_block(end_adj, full_weights, slopes)
    resid_adj = back - lam
    factor_adj, carried_adj = prefix((gains, resid_adj), "layer", combine, identity, True)
    lam = lam + (gains * carried_adj + resid_adj)
    end_adj = jnp.where(is_last, final_adj, from_behind(lam, "layer", -1))
    adjoint = end_adj
    grads = [None] * full_weights.shape[0]
    for j in reversed(range(full_weights.shape[0])):
        adjoint, scaled = back_layer(adjoint, full_weights[j], slopes[j])
        grads[j] = lax.psum_scatter(
            grad_term(kept[j], scaled).astype(jnp.bfloat16), "dp", scatter_dimension=0, tiled=True
        ).astype(jnp.float32)
    return (end_state[None], adjoint[None], jnp.stack(grads), guess[None], lam[None])


def solution(mesh):
    return jax.shard_map(
        local,
        mesh=mesh,
        in_specs=(
            P("dp", None),
            P("layer", "dp", None),
            P("layer", "dp", None),
            P("layer", "dp", None),
            P("layer", None),
            P("layer", None),
            P("dp", None),
        ),
        out_specs=(
            P("layer", "dp", None),
            P("layer", "dp", None),
            P("layer", "dp", None),
            P("layer", "dp", None),
            P("layer", "dp", None),
        ),
        check_vma=False,
    )
```

profile of v0, /device:TPU:12, one launch (start us, length us, event | category | flops | bytes accessed | tf_op | source)
XLA Modules:
  0.0 589.8 jit_solution(7781073490397683310)
XLA Ops:
  7.2 0.7 all-gather.8.cloned.1.call-update
  8.0 3.1 collective-permute-start
  11.1 0.8 fusion.49
  11.9 11.9 %collective-permute-done = f32[128,1024]{1,0:T(8,128)S(1)} collective-permute-done((f32[128,1024]{1,0:T(8,128)}, f32[128,1024]{1,0:T(8,128)S(1)}, u32[]{:S(2)}, u32[]{:S(2)}) %collective-permute-start) | collective-permute-done | bytes 524320 | tf_op jit(solution)/shard_map/ppermute | solution.py:12
  23.7 64.3 %all-gather.8.cloned.1.call-done = bf16[2,1024,1024]{2,1,0:T(8,128)(2,1)} async-done(((bf16[2,32,1024]{2,1,0:T(8,128)(2,1)}), bf16[2,1024,1024]{2,1,0:T(8,128)(2,1)}) %all-gather.8.cloned.1.call-update) | async-done | bytes 4194320 | tf_op jit(solution)/shard_map/all_gather | solution.py:74
  88.0 2.1 fusion.24
  90.2 2.9 fusion.14
  93.2 22.2 %all-gather.3 = f32[16,1,1024]{2,1,0:T(1,128)S(1)} all-gather(f32[1,1,1024]{2,1,0:T(1,128)S(1)} %bitcast.110), channel_id=2, replica_groups=mesh['layer'=16,'dp'=32] {'layer'}, dimensions={0}, use_global_device_ids=true | all-gather | bytes 69632 | tf_op jit(solution)/shard_map/all_gather | solution.py:17
  115.3 59.6 %all-gather.10.cloned.1.call-done = f32[2048,1024]{1,0:T(8,128)} async-done(((f32[128,1024]{1,0:T(8,128)}), f32[2048,1024]{1,0:T(8,128)}) %all-gather.10.cloned.1.call-update) | async-done | bytes 8388624 | tf_op jit(solution)/shard_map/all_gather | solution.py:17
  175.0 24.4 %while.30 = (s32[]{:T(128)}, f32[128,1024]{1,0:T(8,128)S(1)}, s32[]{:T(128)}, f32[16,1,1024]{2,1,0:T(1,128)S(1)}, f32[16,128,1024]{2,1,0:T(8,128)}, /*index=5*/s32[]{:T(128)}, s32[]{:T(128)}) while((s32[]{:T(128)}, f32[128,1024]{1,0:T(8,128)S(1)}, s32[]{:T(128)}, f32[16,1,1024]{2,1,0:T(1,128)S(1)}, f32[16,128,1024]{2,1,0:T(8,128)}, ...), condition=%wide.region_1.2_spmd.clone, body=%wide.region_0.1_spmd.clone.sunk | while | flops 524292 | bytes 1585265 | solution.py:30
  175.0 1.6 fusion.54
  176.6 1.5 fusion.54
  178.1 1.5 fusion.54
  179.6 1.5 fusion.54
  181.1 1.5 fusion.54
  182.7 1.5 fusion.54
  184.2 1.5 fusion.54
  185.7 1.5 fusion.54
  187.2 1.5 fusion.54
  188.8 1.5 fusion.54
  190.3 1.5 fusion.54
  191.8 1.5 fusion.54
  193.3 1.5 fusion.54
  194.9 1.5 fusion.54
  196.4 1.5 fusion.54
  197.9 1.5 fusion.54
  199.4 0.1 add_add_fusion.1
  199.6 3.1 collective-permute-start.1
  202.7 2.8 collective-permute-start.2
  205.5 9.5 %collective-permute-done.1 = f32[128,1024]{1,0:T(8,128)S(1)} collective-permute-done((f32[128,1024]{1,0:T(8,128)S(1)}, f32[128,1024]{1,0:T(8,128)S(1)}, u32[]{:S(2)}, u32[]{:S(2)}) %collective-permute-start.1) | collective-permute-done | bytes 524320 | tf_op jit(solution)/shard_map/ppermute | solution.py:12
  215.0 2.1 multiply_add_fusion
  217.1 0.5 fusion.16
  217.6 1.2 collective-permute-done.2
  218.8 2.1 fusion.18
  220.9 1.7 fusion.29
  222.7 88.4 %all-gather.12.cloned.1.call-done = f32[2048,1024]{1,0:T(8,128)} async-done(((f32[128,1024]{1,0:T(8,128)}), f32[2048,1024]{1,0:T(8,128)}) %all-gather.12.cloned.1.call-update) | async-done | bytes 8388624 | tf_op jit(solution)/shard_map/all_gather | solution.py:17
  311.0 24.4 %while.31 = (s32[]{:T(128)}, f32[128,1024]{1,0:T(8,128)S(1)}, s32[]{:T(128)}, f32[16,1,1024]{2,1,0:T(1,128)S(1)}, f32[16,128,1024]{2,1,0:T(8,128)}, /*index=5*/s32[]{:T(128)}, s32[]{:T(128)}, s32[]{:T(128)}, s32[]{:T(128)}) while((s32[]{:T(128)}, f32[128,1024]{1,0:T(8,128)S(1)}, s32[]{:T(128)}, f32[16,1,1024]{2,1,0:T(1,128)S(1)}, ...), condition=%wide.region_3.4_spmd.clone, body=%wide.region_2.3_spmd.clone.sunk | while | flops 524296 | bytes 1585327 | solution.py:30
  311.1 1.5 fusion.55
  312.6 1.5 fusion.55
  314.1 1.5 fusion.55
  315.6 1.5 fusion.55
  317.2 1.5 fusion.55
  318.7 1.5 fusion.55
  320.2 1.5 fusion.55
  321.7 1.5 fusion.55
  323.3 1.5 fusion.55
  324.8 1.5 fusion.55
  326.3 1.5 fusion.55
  327.9 1.5 fusion.55
  329.4 1.5 fusion.55
  330.9 1.5 fusion.55
  332.5 1.5 fusion.55
  334.0 1.5 fusion.55
  335.6 0.8 copy-done.7
  336.4 2.6 collective-permute-start.3
  339.0 12.9 %collective-permute-done.3 = f32[128,1024]{1,0:T(8,128)S(1)} collective-permute-done((f32[128,1024]{1,0:T(8,128)S(1)}, f32[128,1024]{1,0:T(8,128)S(1)}, u32[]{:S(2)}, u32[]{:S(2)}) %collective-permute-start.3) | collective-permute-done | bytes 524320 | tf_op jit(solution)/shard_map/ppermute | solution.py:12
  351.9 3.0 multiply_convert_fusion
  355.0 2.4 fusion.20
  357.5 2.0 multiply_convert_fusion.1
  359.6 0.9 add_bitcast_fusion
  360.4 3.2 fusion.32
  363.6 106.2 %reduce-scatter.5.cloned.1.call-done = bf16[32,1024]{1,0:T(8,128)(2,1)} async-done(((bf16[1024,1024]{1,0:T(8,128)(2,1)}), bf16[32,1024]{1,0:T(8,128)(2,1)}) %reduce-scatter.5.cloned.1.call-update) | async-done | bytes 65552 | tf_op jit(solution)/shard_map/reduce_scatter | solution.py:103
  469.8 111.9 %reduce-scatter.3.cloned.1.call-done = bf16[32,1024]{1,0:T(8,128)(2,1)} async-done(((bf16[1024,1024]{1,0:T(8,128)(2,1)}), bf16[32,1024]{1,0:T(8,128)(2,1)}) %reduce-scatter.3.cloned.1.call-update) | async-done | bytes 65552 | tf_op jit(solution)/shard_map/reduce_scatter | solution.py:103
  581.7 1.6 maximum_convert_fusion
  (66 shorter events, 0.7 us)
Async XLA Ops:
  7.2 83.0 %copy-start.3 = (f32[1,128,1024]{2,1,0:T(8,128)S(1)}, f32[1,128,1024]{2,1,0:T(8,128)}, u32[]{:S(2)}) copy-start(f32[1,128,1024]{2,1,0:T(8,128)} %param.12) | copy-start | bytes 1572868
  7.2 86.0 %copy-start.10 = (f32[1,1024]{1,0:T(1,128)S(1)}, f32[1,1024]{1,0:T(1,128)}, u32[]{:S(2)}) copy-start(f32[1,1024]{1,0:T(1,128)} %param.16) | copy-start | bytes 12292
  7.2 80.8 %all-gather.8.cloned.1.call-start = ((), (), s32[]{:S(2)}) async-start(), calls=%async_computation.2 | async-start | bytes 4325376 | tf_op jit(solution)/shard_map/all_gather | solution.py:74
  7.9 167.1 %all-gather.10.cloned.1.call-start = ((), (), s32[]{:S(2)}) async-start(), calls=%async_computation.5 | async-start | bytes 8912896 | tf_op jit(solution)/shard_map/all_gather | solution.py:17
  8.0 15.8 %collective-permute-start = (f32[128,1024]{1,0:T(8,128)}, f32[128,1024]{1,0:T(8,128)S(1)}, u32[]{:S(2)}, u32[]{:S(2)}) collective-permute-start(f32[128,1024]{1,0:T(8,128)} %bitcast.100), channel_id=1, source_target_pairs={{0,32},{32,64},{64,96},{96,128},{128,160},{160,192},{192,224},{224... | collective-permute-start | bytes 1572872 | tf_op jit(solution)/shard_map/ppermute | solution.py:12
  93.1 106.3 %copy-start.1 = (f32[128,1024]{1,0:T(8,128)S(1)}, f32[128,1024]{1,0:T(8,128)}, u32[]{:S(2)}) copy-start(f32[128,1024]{1,0:T(8,128)} %fusion.14) | copy-start | bytes 1572868
  93.1 218.0 %all-gather.12.cloned.1.call-start = ((), (), s32[]{:S(2)}) async-start(), calls=%async_computation.6 | async-start | bytes 8912896 | tf_op jit(solution)/shard_map/all_gather | solution.py:17
  175.0 27.7 %copy-start.4 = (f32[1,128,1024]{2,1,0:T(8,128)S(1)}, f32[1,128,1024]{2,1,0:T(8,128)}, u32[]{:S(2)}) copy-start(f32[1,128,1024]{2,1,0:T(8,128)} %param.13) | copy-start | bytes 1572868
  175.0 40.0 %copy-start.5 = (bf16[128,1024]{1,0:T(8,128)(2,1)S(1)}, bf16[128,1024]{1,0:T(8,128)(2,1)}, u32[]{:S(2)}) copy-start(bf16[128,1024]{1,0:T(8,128)(2,1)} %param.11) | copy-start | bytes 786436
  199.5 18.0 %copy-start.6 = (f32[128,1024]{1,0:T(8,128)}, f32[128,1024]{1,0:T(8,128)S(1)}, u32[]{:S(2)}) copy-start(f32[128,1024]{1,0:T(8,128)S(1)} %add_add_fusion.1) | copy-start | bytes 1572868
  199.6 15.4 %collective-permute-start.1 = (f32[128,1024]{1,0:T(8,128)S(1)}, f32[128,1024]{1,0:T(8,128)S(1)}, u32[]{:S(2)}, u32[]{:S(2)}) collective-permute-start(f32[128,1024]{1,0:T(8,128)S(1)} %add_add_fusion.1), channel_id=1, source_target_pairs={{0,32},{32,64},{64,96},{96,128},{128,160},{160,192},{192,224},{224... | collective-permute-start | bytes 1572872 | tf_op jit(solution)/shard_map/ppermute | solution.py:12
  202.7 16.2 %collective-permute-start.2 = (f32[128,1024]{1,0:T(8,128)S(1)}, f32[128,1024]{1,0:T(8,128)}, u32[]{:S(2)}, u32[]{:S(2)}) collective-permute-start(f32[128,1024]{1,0:T(8,128)S(1)} %bitcast.101), channel_id=1, source_target_pairs={{32,0},{64,32},{96,64},{128,96},{160,128},{192,160},{224,192},{256... | collective-permute-start | bytes 1572872 | tf_op jit(solution)/shard_map/ppermute | solution.py:12
  205.4 11.7 %copy-start = (bf16[2,1024,1024]{2,1,0:T(8,128)(2,1)S(1)}, bf16[2,1024,1024]{2,1,0:T(8,128)(2,1)}, u32[]{:S(2)}) copy-start(bf16[2,1024,1024]{2,1,0:T(8,128)(2,1)} %all-gather.8.cloned.1.call-done) | copy-start | bytes 12582916
  205.4 13.4 %copy-start.8 = (bf16[128,1024]{1,0:T(8,128)(2,1)S(1)}, bf16[128,1024]{1,0:T(8,128)(2,1)}, u32[]{:S(2)}) copy-start(bf16[128,1024]{1,0:T(8,128)(2,1)} %param.17) | copy-start | bytes 786436
  222.6 112.9 %copy-start.2 = (f32[128,1024]{1,0:T(8,128)S(1)}, f32[128,1024]{1,0:T(8,128)}, u32[]{:S(2)}) copy-start(f32[128,1024]{1,0:T(8,128)} %fusion.29) | copy-start | bytes 1572868
  222.6 247.2 %reduce-scatter.5.cloned.1.call-start = ((), (), s32[]{:S(2)}) async-start(), calls=%async_computation.4 | async-start | bytes 2162688 | tf_op jit(solution)/shard_map/reduce_scatter | solution.py:103
  335.6 0.8 copy-start.7
  336.4 18.6 %copy-start.9 = (bf16[128,1024]{1,0:T(8,128)(2,1)S(1)}, bf16[128,1024]{1,0:T(8,128)(2,1)}, u32[]{:S(2)}) copy-start(bf16[128,1024]{1,0:T(8,128)(2,1)} %param.17) | copy-start | bytes 786436
  336.4 15.5 %collective-permute-start.3 = (f32[128,1024]{1,0:T(8,128)S(1)}, f32[128,1024]{1,0:T(8,128)S(1)}, u32[]{:S(2)}, u32[]{:S(2)}) collective-permute-start(f32[128,1024]{1,0:T(8,128)S(1)} %add_add_fusion), channel_id=1, source_target_pairs={{32,0},{64,32},{96,64},{128,96},{160,128},{192,160},{224,192},{256... | collective-permute-start | bytes 1572872 | tf_op jit(solution)/shard_map/ppermute | solution.py:12
  355.0 226.7 %reduce-scatter.3.cloned.1.call-start = ((), (), s32[]{:S(2)}) async-start(), calls=%async_computation.3 | async-start | bytes 2162688 | tf_op jit(solution)/shard_map/reduce_scatter | solution.py:103
Sparse Core Ops, SparseCore 0:
  10.1 77.8 all-gather.7
  93.2 81.7 all-gather.9
  222.7 88.2 all-gather.11
  355.1 114.6 reduce-scatter.4
  472.4 109.1 reduce-scatter.2
where the time goes:
time: 592 us; the launch traced here: 590 us
  waiting for transfers between devices  467 us (79%)
  other arithmetic  50.3 us (8%)
  blocking collectives  22.2 us (4%)
  matrix products  22 us (4%)
  between operations  14.1 us (2%)
  starting transfers between devices  11.7 us (2%)
    reduce_scatter x2, waiting for transfers between devices, local(): lax.psum_scatter(grad_term(kept[j], scaled).astype(jnp.bfloat16), 'dp', s...  218 us
    all_gather x2, waiting for transfers between devices, prefix(): everything = jax.tree.map(lambda part: lax.all_gather(part, axis), shard)  148 us
    all_gather x1, waiting for transfers between devices, local(): full_weights = lax.all_gather(weights, 'dp', axis=1, tiled=True)  64.3 us
    select_n x32, other arithmetic, hop(): return jax.tree.map(lambda a, b: jnp.where(reached, a, b), new, before)  47.6 us
    ppermute x4, waiting for transfers between devices, from_behind(): return lax.ppermute(block, axis, route)  35.5 us
    all_gather x1, blocking collectives, prefix(): everything = jax.tree.map(lambda part: lax.all_gather(part, axis), shard)  22.2 us
  transfers between devices with their start and end apart: 9, of which 9 were waited for; matrix products, arithmetic and copies ran while one was open for 2% of the time, Pallas kernels for 0%

commit v1 on v0

--- a/solution.py
+++ b/solution.py
@@ -71,7 +71,9 @@
 
 
 def local(inputs, guess_fwd, guess_adj, weights, biases, gains, cotangent):
-    full_weights = lax.all_gather(weights, "dp", axis=1, tiled=True)
+    full_weights = jnp.concatenate(
+        lax.all_to_all(jnp.stack([weights] * lax.axis_size("dp")), "dp", 0, 0), axis=1
+    )
     count = lax.axis_size("layer")
     index = lax.axis_index("layer")
     is_first = index == 0

time: 592 us -> 720 us (1.22)
  the two profiles are of different devices: /device:TPU:12 before, /device:TPU:2 now
where the time goes in v1:
time: 720 us; the launch traced here: 717 us
  waiting for transfers between devices  570 us (79%)
  other arithmetic  53.4 us (7%)
  starting transfers between devices  27.6 us (4%)
  blocking collectives  23.7 us (3%)
  matrix products  17.1 us (2%)
  between operations  14.1 us (2%)
  local copies, waits for them, and re-layouts  10.3 us (1%)
    reduce_scatter x2, waiting for transfers between devices, local(): lax.psum_scatter(grad_term(kept[j], scaled).astype(jnp.bfloat16), 'dp', s...  216 us
    all_to_all x1, waiting for transfers between devices, local(): lax.all_to_all(jnp.stack([weights] * lax.axis_size('dp')), 'dp', 0, 0)  180 us
    all_gather x2, waiting for transfers between devices, prefix(): everything = jax.tree.map(lambda part: lax.all_gather(part, axis), shard)  151 us
    select_n x32, other arithmetic, hop(): return jax.tree.map(lambda a, b: jnp.where(reached, a, b), new, before)  47.6 us
    all_gather x1, blocking collectives, prefix(): everything = jax.tree.map(lambda part: lax.all_gather(part, axis), shard)  23.7 us
    ppermute x4, waiting for transfers between devices, from_behind(): return lax.ppermute(block, axis, route)  23.6 us
    all_to_all x1, starting transfers between devices, local(): lax.all_to_all(jnp.stack([weights] * lax.axis_size('dp')), 'dp', 0, 0)  15.7 us
  transfers between devices with their start and end apart: 9, of which 8 were waited for; matrix products, arithmetic and copies ran while one was open for 2% of the time, Pallas kernels for 0%

profile of v1, /device:TPU:2, one launch (start us, length us, event | category | flops | bytes accessed | tf_op | source)
XLA Modules:
  0.0 717.5 jit_solution(16984279918396398242)
XLA Ops:
  7.2 3.5 stack.13
  10.6 15.7 %all-to-all-start = ((bf16[32,2,32,1024]{3,2,1,0:T(8,128)(2,1)}), bf16[32,2,32,1024]{3,2,1,0:T(8,128)(2,1)}, u32[]{:S(2)}, u32[]{:S(2)}) async-start(bf16[32,2,32,1024]{3,2,1,0:T(8,128)(2,1)} %stack.13), calls=%async_computation | async-start | bytes 8388608 | tf_op jit(solution)/shard_map/all_to_all | solution.py:75
  26.4 3.4 collective-permute-start
  29.9 180.0 %all-to-all-done = bf16[32,2,32,1024]{3,2,1,0:T(8,128)(2,1)} async-done(((bf16[32,2,32,1024]{3,2,1,0:T(8,128)(2,1)}), bf16[32,2,32,1024]{3,2,1,0:T(8,128)(2,1)}, u32[]{:S(2)}, u32[]{:S(2)}) %all-to-all-start) | async-done | bytes 4194336 | tf_op jit(solution)/shard_map/all_to_all | solution.py:75
  209.9 2.9 fusion.33
  213.3 0.9 copy-done
  214.1 1.3 fusion.13
  215.5 23.7 %all-gather.3 = f32[16,1,1024]{2,1,0:T(1,128)S(1)} all-gather(f32[1,1,1024]{2,1,0:T(1,128)S(1)} %bitcast.67), channel_id=2, replica_groups=mesh['layer'=16,'dp'=32] {'layer'}, dimensions={0}, use_global_device_ids=true | all-gather | bytes 69632 | tf_op jit(solution)/shard_map/all_gather | solution.py:17
  239.2 61.5 %all-gather.7.cloned.1.call-done = f32[2048,1024]{1,0:T(8,128)} async-done(((f32[128,1024]{1,0:T(8,128)}), f32[2048,1024]{1,0:T(8,128)}) %all-gather.7.cloned.1.call-update) | async-done | bytes 8388624 | tf_op jit(solution)/shard_map/all_gather | solution.py:17
  300.8 24.4 %while.30 = (s32[]{:T(128)}, f32[128,1024]{1,0:T(8,128)S(1)}, s32[]{:T(128)}, f32[16,1,1024]{2,1,0:T(1,128)S(1)}, f32[16,128,1024]{2,1,0:T(8,128)}, /*index=5*/s32[]{:T(128)}, s32[]{:T(128)}) while((s32[]{:T(128)}, f32[128,1024]{1,0:T(8,128)S(1)}, s32[]{:T(128)}, f32[16,1,1024]{2,1,0:T(1,128)S(1)}, f32[16,128,1024]{2,1,0:T(8,128)}, ...), condition=%wide.region_1.2_spmd.clone, body=%wide.region_0.1_spmd.clone.sunk | while | flops 524292 | bytes 1585265 | solution.py:30
  300.8 1.5 fusion.47
  302.3 1.5 fusion.47
  303.9 1.5 fusion.47
  305.4 1.5 fusion.47
  306.9 1.5 fusion.47
  308.4 1.5 fusion.47
  310.0 1.5 fusion.47
  311.5 1.5 fusion.47
  313.0 1.5 fusion.47
  314.5 1.5 fusion.47
  316.0 1.5 fusion.47
  317.6 1.5 fusion.47
  319.1 1.5 fusion.47
  320.6 1.5 fusion.47
  322.1 1.5 fusion.47
  323.7 1.5 fusion.47
  325.2 2.0 add_add_fusion.1
  327.1 3.4 collective-permute-start.1
  330.5 2.5 collective-permute-start.2
  333.0 9.7 %collective-permute-done.1 = f32[128,1024]{1,0:T(8,128)S(1)} collective-permute-done((f32[128,1024]{1,0:T(8,128)}, f32[128,1024]{1,0:T(8,128)S(1)}, u32[]{:S(2)}, u32[]{:S(2)}) %collective-permute-start.1) | collective-permute-done | bytes 524320 | tf_op jit(solution)/shard_map/ppermute | solution.py:12
  343.5 0.8 copy-done.2
  345.0 0.9 collective-permute-done.2
  345.9 2.1 fusion.7
  348.0 2.7 fusion.6
  350.8 89.0 %all-gather.9.cloned.1.call-done = f32[2048,1024]{1,0:T(8,128)} async-done(((f32[128,1024]{1,0:T(8,128)}), f32[2048,1024]{1,0:T(8,128)}) %all-gather.9.cloned.1.call-update) | async-done | bytes 8388624 | tf_op jit(solution)/shard_map/all_gather | solution.py:17
  439.8 24.4 %while.31 = (s32[]{:T(128)}, f32[128,1024]{1,0:T(8,128)S(1)}, s32[]{:T(128)}, f32[16,1,1024]{2,1,0:T(1,128)S(1)}, f32[16,128,1024]{2,1,0:T(8,128)}, /*index=5*/s32[]{:T(128)}, s32[]{:T(128)}, s32[]{:T(128)}, s32[]{:T(128)}) while((s32[]{:T(128)}, f32[128,1024]{1,0:T(8,128)S(1)}, s32[]{:T(128)}, f32[16,1,1024]{2,1,0:T(1,128)S(1)}, ...), condition=%wide.region_3.4_spmd.clone, body=%wide.region_2.3_spmd.clone.sunk | while | flops 524296 | bytes 1585327 | solution.py:30
  439.8 1.5 fusion.48
  441.3 1.5 fusion.48
  442.9 1.5 fusion.48
  444.4 1.5 fusion.48
  445.9 1.5 fusion.48
  447.4 1.5 fusion.48
  449.0 1.5 fusion.48
  450.5 1.5 fusion.48
  452.0 1.5 fusion.48
  453.6 1.5 fusion.48
  455.1 1.5 fusion.48
  456.6 1.5 fusion.48
  458.1 1.5 fusion.48
  459.7 1.5 fusion.48
  461.2 1.5 fusion.48
  462.7 1.5 fusion.48
  464.2 1.4 add_add_fusion
  466.4 2.5 collective-permute-start.3
  468.9 12.9 %collective-permute-done.3 = f32[128,1024]{1,0:T(8,128)S(1)} collective-permute-done((f32[128,1024]{1,0:T(8,128)S(1)}, f32[128,1024]{1,0:T(8,128)S(1)}, u32[]{:S(2)}, u32[]{:S(2)}) %collective-permute-start.3) | collective-permute-done | bytes 524320 | tf_op jit(solution)/shard_map/ppermute | solution.py:12
  481.8 2.1 multiply_convert_fusion
  484.0 2.5 fusion.4
  486.5 0.8 copy-done.7
  487.3 2.1 multiply_convert_fusion.1
  489.4 0.9 add_bitcast_fusion
  490.3 3.0 fusion.3
  493.3 104.2 %reduce-scatter.5.cloned.1.call-done = bf16[32,1024]{1,0:T(8,128)(2,1)} async-done(((bf16[1024,1024]{1,0:T(8,128)(2,1)}), bf16[32,1024]{1,0:T(8,128)(2,1)}) %reduce-scatter.5.cloned.1.call-update) | async-done | bytes 65552 | tf_op jit(solution)/shard_map/reduce_scatter | solution.py:105
  597.5 111.9 %reduce-scatter.3.cloned.1.call-done = bf16[32,1024]{1,0:T(8,128)(2,1)} async-done(((bf16[1024,1024]{1,0:T(8,128)(2,1)}), bf16[32,1024]{1,0:T(8,128)(2,1)}) %reduce-scatter.3.cloned.1.call-update) | async-done | bytes 65552 | tf_op jit(solution)/shard_map/reduce_scatter | solution.py:105
  709.4 1.6 maximum_convert_fusion
  (79 shorter events, 3.2 us)
Async XLA Ops:
  10.6 15.8 %copy-start.13 = (f32[1,128,1024]{2,1,0:T(8,128)S(1)}, f32[1,128,1024]{2,1,0:T(8,128)}, u32[]{:S(2)}) copy-start(f32[1,128,1024]{2,1,0:T(8,128)} %param.12) | copy-start | bytes 1572868
  10.6 19.2 %copy-start.16 = (f32[2,1024]{1,0:T(2,128)S(1)}, f32[2,1024]{1,0:T(2,128)}, u32[]{:S(2)}) copy-start(f32[2,1024]{1,0:T(2,128)} %param.15) | copy-start | bytes 24580
  10.6 199.3 %all-to-all-start = ((bf16[32,2,32,1024]{3,2,1,0:T(8,128)(2,1)}), bf16[32,2,32,1024]{3,2,1,0:T(8,128)(2,1)}, u32[]{:S(2)}, u32[]{:S(2)}) async-start(bf16[32,2,32,1024]{3,2,1,0:T(8,128)(2,1)} %stack.13), calls=%async_computation | async-start | bytes 8388608 | tf_op jit(solution)/shard_map/all_to_all | solution.py:75
  26.4 274.4 %all-gather.7.cloned.1.call-start = ((), (), s32[]{:S(2)}) async-start(), calls=%async_computation.5 | async-start | bytes 8912896 | tf_op jit(solution)/shard_map/all_gather | solution.py:17
  26.4 186.3 %collective-permute-start = (f32[128,1024]{1,0:T(8,128)S(1)}, f32[128,1024]{1,0:T(8,128)S(1)}, u32[]{:S(2)}, u32[]{:S(2)}) collective-permute-start(f32[128,1024]{1,0:T(8,128)S(1)} %bitcast.59), channel_id=1, source_target_pairs={{0,32},{32,64},{64,96},{96,128},{128,160},{160,192},{192,224},{224... | collective-permute-start | bytes 1572872 | tf_op jit(solution)/shard_map/ppermute | solution.py:12
  209.9 2.9 copy-start.10
  212.8 1.4 copy-start
  214.1 1.4 copy-start.15
  215.4 224.4 %all-gather.9.cloned.1.call-start = ((), (), s32[]{:S(2)}) async-start(), calls=%async_computation.6 | async-start | bytes 8912896 | tf_op jit(solution)/shard_map/all_gather | solution.py:17
  300.8 24.4 %copy-start.8 = (f32[128,1024]{1,0:T(8,128)S(1)}, f32[128,1024]{1,0:T(8,128)}, u32[]{:S(2)}) copy-start(f32[128,1024]{1,0:T(8,128)} %fusion.13) | copy-start | bytes 1572868
  327.1 15.6 %collective-permute-start.1 = (f32[128,1024]{1,0:T(8,128)}, f32[128,1024]{1,0:T(8,128)S(1)}, u32[]{:S(2)}, u32[]{:S(2)}) collective-permute-start(f32[128,1024]{1,0:T(8,128)} %add_add_fusion.1), channel_id=1, source_target_pairs={{0,32},{32,64},{64,96},{96,128},{128,160},{160,192},{192,224},{224... | collective-permute-start | bytes 1572872 | tf_op jit(solution)/shard_map/ppermute | solution.py:12
  330.5 15.4 %collective-permute-start.2 = (f32[128,1024]{1,0:T(8,128)}, f32[128,1024]{1,0:T(8,128)}, u32[]{:S(2)}, u32[]{:S(2)}) collective-permute-start(f32[128,1024]{1,0:T(8,128)} %bitcast.10), channel_id=1, source_target_pairs={{32,0},{64,32},{96,64},{128,96},{160,128},{192,160},{224,192},{256... | collective-permute-start | bytes 1572872 | tf_op jit(solution)/shard_map/ppermute | solution.py:12
  342.8 0.7 copy-start.11
  342.8 1.7 copy-start.1
  343.5 0.8 copy-start.2
  343.5 4.5 copy-start.5
  343.5 2.4 copy-start.9
  350.7 246.8 %reduce-scatter.5.cloned.1.call-start = ((), (), s32[]{:S(2)}) async-start(), calls=%async_computation.4 | async-start | bytes 2162688 | tf_op jit(solution)/shard_map/reduce_scatter | solution.py:105
  464.2 17.6 %copy-start.3 = (f32[128,1024]{1,0:T(8,128)S(1)}, f32[128,1024]{1,0:T(8,128)}, u32[]{:S(2)}) copy-start(f32[128,1024]{1,0:T(8,128)} %copy-done.2) | copy-start | bytes 1572868
  465.6 0.8 copy-start.14
  466.4 15.4 %collective-permute-start.3 = (f32[128,1024]{1,0:T(8,128)S(1)}, f32[128,1024]{1,0:T(8,128)S(1)}, u32[]{:S(2)}, u32[]{:S(2)}) collective-permute-start(f32[128,1024]{1,0:T(8,128)S(1)} %add_add_fusion), channel_id=1, source_target_pairs={{32,0},{64,32},{96,64},{128,96},{160,128},{192,160},{224,192},{256... | collective-permute-start | bytes 1572872 | tf_op jit(solution)/shard_map/ppermute | solution.py:12
  483.9 225.4 %reduce-scatter.3.cloned.1.call-start = ((), (), s32[]{:S(2)}) async-start(), calls=%async_computation.3 | async-start | bytes 2162688 | tf_op jit(solution)/shard_map/reduce_scatter | solution.py:105
  484.0 3.4 copy-start.6
  484.0 3.3 copy-start.12
  486.5 0.8 copy-start.7
  487.3 2.1 copy-start.4
Sparse Core Ops, SparseCore 0:
  215.5 85.1 all-gather.6
  350.8 88.9 all-gather.8
  484.1 113.3 reduce-scatter.4
  600.1 109.1 reduce-scatter.2
